TPU v7x, 128 devices: a whole 4x4x4 slice. The times are simulated.
128 devices in a mesh: fsdp: 32 (over z, y, core), slide: 4 (over x).
Axes of the slice: x: 4, y: 4, z: 4, core: 2. Of those that a mesh axis runs over, the one named last changes fastest.
Arguments:
- tiles: bfloat16 [65536, 1536], P(('slide', 'fsdp')), parts along dimension 0, may hold values from -6 to 6
- tile_cell: int32 [65536], P('slide'), parts along dimension 0, may hold values from 0 to 16383, as said below
- tissue: int32 [256, 256], P('slide'), parts along dimension 0, may hold values 0 or 1
- norm_gain: float32 [2, 1536], replicated, may hold values from 0.5 to 1.5
- qk_gain: float32 [2, 2, 64], replicated, may hold values from 0.5 to 4
- row_qkv: bfloat16 [1536, 4608], P(None, 'fsdp'), may hold values from -0.15625 to 0.15625
- row_out: bfloat16 [1536, 1536], P(None, 'fsdp'), may hold values from -0.15625 to 0.15625
- col_qkv: bfloat16 [1536, 4608], P(None, 'fsdp'), may hold values from -0.15625 to 0.15625
- col_out: bfloat16 [1536, 1536], P(None, 'fsdp'), may hold values from -0.15625 to 0.15625
Outputs:
- encoded: bfloat16 [256, 256, 1536], P('slide', 'fsdp'), parts along dimension 0
There are 4 independent parts, one for each index of `slide`. A program takes and returns all parts, laid end to end along the dimension named above; an argument that names none is the same for every part. Nothing has to cross between parts.
Inputs may be any that keep to these rules, and one draw needn't show every extreme that they name: Slots d * 512 + b * 16 up to d * 512 + (b + 1) * 16 - 1 hold tiles of grid rows b * 2 to (b + 1) * 2 - 1; tile_cell names every grid cell exactly once.
All inputs are finite; a program needn't handle non-finite values.
Results may differ from a plain program's by a relative error of at most 0.02.
The roundings to bfloat16 on the way count: a program that leaves them out, or rounds other values in their place, can miss the bound.
Values may be sent and summed in bfloat16 or wider, within the bound.
No kernel may reach another device: no remote copies, remote signals or barrier semaphores. Data moves between devices by JAX's collectives and lax.ppermute only.
A program may use at most 256 MiB of HBM per device.

v0:
```python
import jax
import jax.numpy as jnp
from jax import lax
from jax.sharding import PartitionSpec as P

HEADS = 24


EPS = 1e-06


def rms_norm(grid, gain):
    values = grid.astype(jnp.float32)
    scale = lax.rsqrt(jnp.mean(values * values, axis=-1, keepdims=True) + EPS)
    return (values * scale * gain).astype(jnp.bfloat16)


def head_norm(values, gain):
    scale = lax.rsqrt(jnp.mean(values * values, axis=-1, keepdims=True) + EPS)
    return values * scale * gain


def rotate(values, rows_pos, cols_pos):
    quarter = values.shape[-1] // 4
    freq = 10000.0 ** (-jnp.arange(quarter).astype(jnp.float32) / quarter)

    def turn(part, position):
        angle = position.astype(jnp.float32)[..., None, None] * freq
        cosine = jnp.cos(angle)
        sine = jnp.sin(angle)
        first = part[..., :quarter]
        second = part[..., quarter:]
        return jnp.concatenate(
            [first * cosine - second * sine, first * sine + second * cosine], axis=-1
        )

    half = 2 * quarter
    return jnp.concatenate(
        [turn(values[..., :half], rows_pos), turn(values[..., half:], cols_pos)], axis=-1
    )


def attend(qkv, gains, rows_pos, cols_pos, keys_live, column, heads):
    width = qkv.shape[-1] // 3
    size = width // heads
    shape = qkv.shape[:-1] + (heads, size)
    query = qkv[..., :width].reshape(shape).astype(jnp.float32)
    key = qkv[..., width : 2 * width].reshape(shape).astype(jnp.float32)
    value = qkv[..., 2 * width :].reshape(shape)
    query = rotate(head_norm(query, gains[0]), rows_pos, cols_pos).astype(jnp.bfloat16)
    key = rotate(head_norm(key, gains[1]), rows_pos, cols_pos).astype(jnp.bfloat16)
    if column:
        score_form = "lbhd,mbhd->bhlm"
        mix_form = "bhlm,mbhd->lbhd"
        live = keys_live.T
    else:
        score_form = "blhd,bmhd->bhlm"
        mix_form = "bhlm,bmhd->blhd"
        live = keys_live
    scores = jnp.einsum(score_form, query, key, preferred_element_type=jnp.float32) * size ** (-0.5)
    length = scores.shape[-1]
    diagonal = jnp.arange(length)[:, None] == jnp.arange(length)[None, :]
    allow = (live[:, None, None, :] > 0) | diagonal[None, None]
    scores = jnp.where(allow, scores, -1e30)
    top = jnp.max(scores, axis=-1, keepdims=True)
    weights = jnp.exp(scores - top)
    total = jnp.sum(weights, axis=-1)
    mixed = jnp.einsum(
        mix_form, weights.astype(jnp.bfloat16), value, preferred_element_type=jnp.float32
    )
    if column:
        total = total.transpose(2, 0, 1)
    else:
        total = total.transpose(0, 2, 1)
    return (mixed / total[..., None]).reshape(qkv.shape[:-1] + (width,)).astype(jnp.bfloat16)


def project_qkv(normed, weight):

    def multiply(piece, start):
        return jnp.dot(normed, piece, preferred_element_type=jnp.float32)

    return multiply(lax.all_gather(weight, "fsdp", axis=1, tiled=True), jnp.int32(0)).astype(
        jnp.bfloat16
    )


def project_out(mixed, weight):

    def multiply(piece, start):
        return jnp.dot(mixed, piece, preferred_element_type=jnp.float32)

    return multiply(lax.all_gather(weight, "fsdp", axis=1, tiled=True), jnp.int32(0))


def on_device(tiles, tile_cell, tissue, norm_gain, qk_gain, row_qkv, row_out, col_qkv, col_out):
    count = lax.axis_size("fsdp")
    index = lax.axis_index("fsdp")
    width = tiles.shape[1]
    tok_dev = tiles.shape[0]
    slots = tok_dev // count
    grid_rows = tissue.shape[0]
    columns = tissue.shape[1]
    rows_dev = grid_rows // count
    cols_dev = columns // count
    arrived = lax.all_to_all(
        tiles.reshape(count, slots, width), "fsdp", split_axis=0, concat_axis=0, tiled=True
    )
    table_cell = lax.dynamic_index_in_dim(
        tile_cell.reshape(count, count, slots), index, 1, keepdims=False
    )
    row_base = index * rows_dev
    local_cells = (table_cell - row_base * columns).reshape(-1)
    grid = (
        jnp.zeros((tok_dev, width), jnp.bfloat16)
        .at[local_cells]
        .set(arrived.reshape(tok_dev, width))
    )
    rows_pos = row_base + lax.broadcasted_iota(jnp.int32, (rows_dev, columns), 0)
    cols_pos = lax.broadcasted_iota(jnp.int32, (rows_dev, columns), 1)
    live_rows = lax.dynamic_slice_in_dim(tissue, row_base, rows_dev, 0)
    qkv = project_qkv(rms_norm(grid, norm_gain[0]), row_qkv).reshape(rows_dev, columns, 3 * width)
    mixed = attend(qkv, qk_gain[0], rows_pos, cols_pos, live_rows, False, HEADS)
    hidden = grid.astype(jnp.float32) + project_out(mixed.reshape(tok_dev, width), row_out)
    hidden = hidden.astype(jnp.bfloat16).reshape(rows_dev, columns, width)
    turned = lax.all_to_all(hidden, "fsdp", split_axis=1, concat_axis=0, tiled=True)
    col_base = index * cols_dev
    rows_pos_col = lax.broadcasted_iota(jnp.int32, (grid_rows, cols_dev), 0)
    cols_pos_col = col_base + lax.broadcasted_iota(jnp.int32, (grid_rows, cols_dev), 1)
    live_cols = lax.dynamic_slice_in_dim(tissue, col_base, cols_dev, 1)
    flat = turned.reshape(grid_rows * cols_dev, width)
    qkv_col = project_qkv(rms_norm(flat, norm_gain[1]), col_qkv).reshape(
        grid_rows, cols_dev, 3 * width
    )
    mixed_col = attend(qkv_col, qk_gain[1], rows_pos_col, cols_pos_col, live_cols, True, HEADS)
    result = flat.astype(jnp.float32) + project_out(
        mixed_col.reshape(grid_rows * cols_dev, width), col_out
    )
    return result.astype(jnp.bfloat16).reshape(grid_rows, cols_dev, width)


def solution(mesh):
    return jax.shard_map(
        on_device,
        mesh=mesh,
        in_specs=(
            P(("slide", "fsdp"), None),
            P("slide"),
            P("slide", None),
            P(),
            P(),
            P(None, "fsdp"),
            P(None, "fsdp"),
            P(None, "fsdp"),
            P(None, "fsdp"),
        ),
        out_specs=P("slide", "fsdp", None),
        check_vma=False,
    )
```

profile of v0, /device:TPU:1, one launch (start us, length us, event | category | flops | bytes accessed | tf_op | source)
XLA Modules:
  0.0 325.8 jit_solution(16817885451585981338)
XLA Ops:
  8.8 9.6 %all-to-all-start = ((bf16[32,16,1536]{2,1,0:T(8,128)(2,1)}), bf16[32,16,1536]{2,1,0:T(8,128)(2,1)S(1)}, u32[]{:S(2)}, u32[]{:S(2)}) async-start(bf16[32,16,1536]{2,1,0:T(8,128)(2,1)} %bitcast.73), calls=%async_computation | async-start | bytes 3145728 | tf_op jit(solution)/shard_map/all_to_all | solution.py:106
  19.3 27.7 %all-to-all-done = bf16[32,16,1536]{2,1,0:T(8,128)(2,1)S(1)} async-done(((bf16[32,16,1536]{2,1,0:T(8,128)(2,1)}), bf16[32,16,1536]{2,1,0:T(8,128)(2,1)S(1)}, u32[]{:S(2)}, u32[]{:S(2)}) %all-to-all-start) | async-done | bytes 1572896 | tf_op jit(solution)/shard_map/all_to_all | solution.py:106
  46.9 3.4 %scatter_custom_fusion = bf16[512,1536]{1,0:T(8,128)(2,1)S(1)} fusion(s32[512]{0:T(512)S(1)} %bitcast.80, bf16[512,1536]{1,0:T(8,128)(2,1)S(1)} %bitcast.74, bf16[]{:T(256)} %constant.19.clone.1), kind=kCustom, calls=%fused_computation.104 | custom fusion | bytes 1572866 | tf_op jit(solution)/shard_map/scatter | solution.py:117
  50.8 38.5 %all-gather.5.cloned.1.call-done = bf16[1536,4608]{0,1:T(8,128)(2,1)} async-done(((bf16[1536,144]{0,1:T(8,128)(2,1)}), bf16[1536,4608]{0,1:T(8,128)(2,1)}) %all-gather.5.cloned.1.call-update) | async-done | bytes 14155792 | tf_op jit(solution)/shard_map/all_gather | solution.py:83
  89.3 11.4 %convolution_convert_fusion.1 = bf16[512,4608]{1,0:T(8,128)(2,1)S(1)} fusion(bf16[1536,4608]{0,1:T(8,128)(2,1)} %all-gather.5.cloned.1.call-done, bf16[512,1536]{1,0:T(8,128)(2,1)S(1)} %scatter_custom_fusion, f32[1536]{0:T(1024)S(1)} %get-tuple-element.6, f32[512]{0:T(512)S(1)} %add_rsqrt_fusion.5), kind=kOutput, calls=%fused_computation.7 | convolution fusion | flops 7253262336 | bytes 20455424 | tf_op jit(solution)/shard_map/dot_general | solution.py:81
  122.0 3.4 %fusion.38 = bf16[2,256,24,64]{1,3,2,0:T(8,128)(2,1)S(1)} fusion(bf16[2,256,24,64]{1,3,2,0:T(8,128)(2,1)S(1)} %bitcast.75, f32[2,24,256,256]{2,3,1,0:T(8,128)S(1)} %get-tuple-element.54, f32[2,24,256]{2,1,0:T(8,128)S(1)} %get-tuple-element.53, pred[2,256,256]{1,2,0:T(8,128)(4,1)S(1)} %broadcast_or_fusion, f32[2,256,24]{1,2,0:T(8,128)S(1)} %bitcast.79), kind=kOutput, calls=%fused_computation.62 | convolution fusion | flops 416808960 | bytes 15958016 | tf_op jit(solution)/shard_map/bhlm,bmhd->blhd/dot_general | solution.py:68
  127.5 10.3 %all-gather.7.cloned.1.call-done = bf16[1536,1536]{0,1:T(8,128)(2,1)} async-done(((bf16[1536,48]{0,1:T(8,128)(2,1)}), bf16[1536,1536]{0,1:T(8,128)(2,1)}) %all-gather.7.cloned.1.call-update) | async-done | bytes 4718608 | tf_op jit(solution)/shard_map/all_gather | solution.py:93
  137.8 5.0 %fusion.44 = bf16[512,1536]{1,0:T(8,128)(2,1)S(1)} fusion(bf16[512,1536]{0,1:T(8,128)(2,1)S(1)} %bitcast.76, bf16[1536,1536]{0,1:T(8,128)(2,1)} %all-gather.7.cloned.1.call-done, bf16[512,1536]{1,0:T(8,128)(2,1)S(1)} %copy-done.5), kind=kOutput, calls=%fused_computation.73 | convolution fusion | flops 2418278400 | bytes 9437184 | tf_op jit(solution)/shard_map/dot_general | solution.py:91
  145.5 5.3 %all-to-all-start.1 = ((bf16[2,256,1536]{2,0,1:T(2,128)(2,1)}), bf16[2,256,1536]{2,0,1:T(2,128)(2,1)S(1)}, u32[]{:S(2)}, u32[]{:S(2)}) async-start(bf16[2,256,1536]{2,0,1:T(2,128)(2,1)} %copy.69), calls=%async_computation.1 | async-start | bytes 3145728 | tf_op jit(solution)/shard_map/all_to_all | solution.py:126
  153.2 25.3 %all-to-all-done.1 = bf16[2,256,1536]{2,0,1:T(2,128)(2,1)S(1)} async-done(((bf16[2,256,1536]{2,0,1:T(2,128)(2,1)}), bf16[2,256,1536]{2,0,1:T(2,128)(2,1)S(1)}, u32[]{:S(2)}, u32[]{:S(2)}) %all-to-all-start.1) | async-done | bytes 1572896 | tf_op jit(solution)/shard_map/all_to_all | solution.py:126
  185.0 34.7 %all-gather.9.cloned.1.call-done = bf16[1536,4608]{0,1:T(8,128)(2,1)} async-done(((bf16[1536,144]{0,1:T(8,128)(2,1)}), bf16[1536,4608]{0,1:T(8,128)(2,1)}) %all-gather.9.cloned.1.call-update) | async-done | bytes 14155792 | tf_op jit(solution)/shard_map/all_gather | solution.py:83
  219.6 10.7 %fusion.3 = bf16[64,8,4608]{2,1,0:T(8,128)(2,1)S(1)} fusion(bf16[512,1536]{1,0:T(8,128)(2,1)S(1)} %fusion.37, bf16[1536,4608]{0,1:T(8,128)(2,1)} %all-gather.9.cloned.1.call-done), kind=kOutput, calls=%fused_computation.8 | convolution fusion | flops 7250116608 | bytes 20447232 | tf_op jit(solution)/shard_map/dot_general | solution.py:81
  230.4 3.2 fusion.77
  233.6 5.5 %reshape.257 = f32[64,8,24,64]{3,2,1,0:T(8,128)} reshape(f32[64,8,1536]{2,1,0:T(8,128)} %get-tuple-element.20) | data formatting | bytes 6291456 | tf_op jit(solution)/shard_map/convert_element_type | solution.py:48
  239.1 5.2 %multiply_reduce_fusion = f32[64,8,24]{2,1,0:T(8,128)} fusion(f32[64,8,24,64]{3,2,1,0:T(8,128)} %reshape.257), kind=kLoop, calls=%fused_computation.22 | loop fusion | flops 1560576 | bytes 3194880 | tf_op jit(solution)/shard_map/reduce_sum | solution.py:19
  246.0 3.5 %reshape.256 = f32[64,8,24,64]{3,2,1,0:T(8,128)} reshape(f32[64,8,1536]{2,1,0:T(8,128)S(1)} %get-tuple-element.21) | data formatting | bytes 6291456 | tf_op jit(solution)/shard_map/convert_element_type | solution.py:47
  249.5 5.0 %multiply_reduce_fusion.1 = f32[64,8,24]{2,1,0:T(8,128)S(1)} fusion(f32[64,8,24,64]{3,2,1,0:T(8,128)} %reshape.256), kind=kLoop, calls=%fused_computation.27 | loop fusion | flops 1560576 | bytes 3194880 | tf_op jit(solution)/shard_map/reduce_sum | solution.py:19
  258.0 9.4 %fusion.7 = (f32[64,8,24,64]{3,0,2,1:T(8,128)S(1)}, f32[64,8,24,64]{3,0,2,1:T(8,128)S(1)}) fusion(f32[64,8,24,64]{3,2,1,0:T(8,128)} %reshape.257, f32[64]{0:T(128)S(1)} %get-tuple-element.37, f32[64,8,24]{0,2,1:T(8,128)S(1)} %add_rsqrt_fusion.1, f32[64]{0:T(128)S(1)} %get-tuple-element.40, f32[64,8,24]{0,2,1:T(8,128)S(1)} %add_rsqrt_fusion.2, ...), kind=kLoop, calls=%fused_computation.13 | loop fusion | flops 3145728 | bytes 12681728 | tf_op jit(solution)/shard_map/mul | solution.py:20
  267.4 8.0 %subtract_convert_fusion.3 = (bf16[64,8,24,16]{3,0,2,1:T(8,128)(2,1)}, bf16[64,8,24,16]{3,0,2,1:T(8,128)(2,1)}, bf16[64,8,24,16]{3,0,2,1:T(8,128)(2,1)}, bf16[64,8,24,16]{3,0,2,1:T(8,128)(2,1)}) fusion(f32[64,8,24,64]{3,0,2,1:T(8,128)S(1)} %get-tuple-element.58, f32[64,8,16]{2,0,1:T(8,128)S(1)} %copy-done.8, f32[64,8,16]{2,0,1:T(8,128)S(1)} %get-tuple-element.43, ...), kind=kLoop, calls=%fused_computation.26 | loop fusion | flops 3145728 | bytes 4849664 | tf_op jit(solution)/shard_map/convert.11
  275.4 7.8 %subtract_convert_fusion.1 = (bf16[64,8,24,16]{3,0,2,1:T(8,128)(2,1)}, bf16[64,8,24,16]{3,0,2,1:T(8,128)(2,1)}, bf16[64,8,24,16]{3,0,2,1:T(8,128)(2,1)}, bf16[64,8,24,16]{3,0,2,1:T(8,128)(2,1)}) fusion(f32[64,8,24,64]{3,0,2,1:T(8,128)S(1)} %get-tuple-element.57, f32[64,8,16]{2,0,1:T(8,128)S(1)} %copy-done.8, f32[64,8,16]{2,0,1:T(8,128)S(1)} %get-tuple-element.43, ...), kind=kLoop, calls=%fused_computation.21 | loop fusion | flops 3145728 | bytes 4849664 | tf_op jit(solution)/shard_map/convert.7
  283.2 13.0 %fusion.13 = (f32[8,24,64]{2,1,0:T(8,128)S(1)}, f32[8,24,64,64]{2,3,1,0:T(8,128)S(1)}) fusion(pred[8,64,64]{1,2,0:T(8,128)(4,1)S(1)} %broadcast_or_fusion.1, bf16[64,8,24,16]{3,0,2,1:T(8,128)(2,1)} %get-tuple-element.15, bf16[64,8,24,16]{3,0,2,1:T(8,128)(2,1)} %get-tuple-element.16, bf16[64,8,24,16]{3,0,2,1:T(8,128)(2,1)} %get-tuple-element.8, ...), kind=kOutput, calls=%fused_computation.32 | convolution fusion | flops 115593216 | bytes 6373376 | tf_op jit(solution)/shard_map/lbhd,mbhd->bhlm/dot_general | solution.py:60
  301.4 5.3 %copy.80 = bf16[64,8,24,64]{3,2,1,0:T(8,128)(2,1)} copy(bf16[64,8,24,64]{0,3,2,1:T(8,128)(2,1)} %fusion.6) | data formatting | bytes 3145728 | tf_op jit(solution)/shard_map/convert_element_type | solution.py:75
  306.7 5.5 %convert_element_type.211 = bf16[512,1536]{1,0:T(8,128)(2,1)} reshape(bf16[64,8,24,64]{3,2,1,0:T(8,128)(2,1)} %copy.80) | data formatting | bytes 3145728 | tf_op jit(solution)/shard_map/convert_element_type | solution.py:75
  312.2 6.6 %fusion.45 = bf16[64,8,1536]{2,1,0:T(8,128)(2,1)} fusion(f32[512,1536]{1,0:T(8,128)S(1)} %bitcast.69, bf16[512,1536]{1,0:T(8,128)(2,1)} %convert_element_type.211, bf16[1536,1536]{0,1:T(8,128)(2,1)} %all-gather.11.cloned.1.call-done), kind=kOutput, calls=%fused_computation.74 | convolution fusion | flops 2417491968 | bytes 11010048 | tf_op jit(solution)/shard_map/dot_general | solution.py:91
  (95 shorter events, 48.4 us)
Async XLA Ops:
  6.5 11.9 %copy-start.13 = (s32[16384]{0:T(1024)S(1)}, s32[16384]{0:T(1024)}, u32[]{:S(2)}) copy-start(s32[16384]{0:T(1024)} %param.10) | copy-start | bytes 196612
  6.5 12.2 %copy-start.14 = (s32[64,256]{1,0:T(8,128)S(1)}, s32[64,256]{1,0:T(8,128)}, u32[]{:S(2)}) copy-start(s32[64,256]{1,0:T(8,128)} %param.11) | copy-start | bytes 196612
  6.5 12.3 %copy-start.15 = (f32[2,1536]{1,0:T(2,128)S(1)}, f32[2,1536]{1,0:T(2,128)}, u32[]{:S(2)}) copy-start(f32[2,1536]{1,0:T(2,128)} %param.12) | copy-start | bytes 36868
  6.5 12.3 %copy-start.16 = (f32[2,2,64]{2,1,0:T(2,128)S(1)}, f32[2,2,64]{2,1,0:T(2,128)}, u32[]{:S(2)}) copy-start(f32[2,2,64]{2,1,0:T(2,128)} %param.13) | copy-start | bytes 3076
  6.5 82.7 %all-gather.5.cloned.1.call-start = ((), (), s32[]{:S(2)}) async-start(), calls=%async_computation.2 | async-start | bytes 14598144 | tf_op jit(solution)/shard_map/all_gather | solution.py:83
  7.3 130.5 %all-gather.7.cloned.1.call-start = ((), (), s32[]{:S(2)}) async-start(), calls=%async_computation.3 | async-start | bytes 4866048 | tf_op jit(solution)/shard_map/all_gather | solution.py:93
  8.0 211.6 %all-gather.9.cloned.1.call-start = ((), (), s32[]{:S(2)}) async-start(), calls=%async_computation.4 | async-start | bytes 14598144 | tf_op jit(solution)/shard_map/all_gather | solution.py:83
  8.8 38.2 %all-to-all-start = ((bf16[32,16,1536]{2,1,0:T(8,128)(2,1)}), bf16[32,16,1536]{2,1,0:T(8,128)(2,1)S(1)}, u32[]{:S(2)}, u32[]{:S(2)}) async-start(bf16[32,16,1536]{2,1,0:T(8,128)(2,1)} %bitcast.73), calls=%async_computation | async-start | bytes 3145728 | tf_op jit(solution)/shard_map/all_to_all | solution.py:106
  50.4 50.3 %copy-start.4 = (bf16[512,1536]{1,0:T(8,128)(2,1)}, bf16[512,1536]{1,0:T(8,128)(2,1)S(1)}, u32[]{:S(2)}) copy-start(bf16[512,1536]{1,0:T(8,128)(2,1)S(1)} %scatter_custom_fusion) | copy-start | bytes 4718596
  111.3 2.9 copy-start
  118.9 3.1 copy-start.11
  125.5 12.3 %copy-start.5 = (bf16[512,1536]{1,0:T(8,128)(2,1)S(1)}, bf16[512,1536]{1,0:T(8,128)(2,1)}, u32[]{:S(2)}) copy-start(bf16[512,1536]{1,0:T(8,128)(2,1)} %copy-done.4) | copy-start | bytes 4718596
  145.5 33.0 %all-to-all-start.1 = ((bf16[2,256,1536]{2,0,1:T(2,128)(2,1)}), bf16[2,256,1536]{2,0,1:T(2,128)(2,1)S(1)}, u32[]{:S(2)}, u32[]{:S(2)}) async-start(bf16[2,256,1536]{2,0,1:T(2,128)(2,1)} %copy.69), calls=%async_computation.1 | async-start | bytes 3145728 | tf_op jit(solution)/shard_map/all_to_all | solution.py:126
  150.9 161.3 %all-gather.11.cloned.1.call-start = ((), (), s32[]{:S(2)}) async-start(), calls=%async_computation.5 | async-start | bytes 4866048 | tf_op jit(solution)/shard_map/all_gather | solution.py:93
  249.5 5.1 %copy-start.6 = (bf16[64,8,1536]{2,1,0:T(8,128)(2,1)S(1)}, bf16[64,8,1536]{2,1,0:T(8,128)(2,1)}, u32[]{:S(2)}) copy-start(bf16[64,8,1536]{2,1,0:T(8,128)(2,1)} %get-tuple-element.19) | copy-start | bytes 4718596
  254.5 3.4 %copy-start.12 = (f32[64,8,24]{0,2,1:T(8,128)S(1)}, f32[64,8,24]{0,2,1:T(8,128)}, u32[]{:S(2)}) copy-start(f32[64,8,24]{0,2,1:T(8,128)} %copy.77) | copy-start | bytes 147460
  258.0 9.5 %copy-start.8 = (f32[64,8,16]{2,0,1:T(8,128)S(1)}, f32[64,8,16]{2,0,1:T(8,128)}, u32[]{:S(2)}) copy-start(f32[64,8,16]{2,0,1:T(8,128)} %get-tuple-element.44) | copy-start | bytes 98308
  258.0 9.5 %copy-start.9 = (f32[64,8,16]{2,0,1:T(8,128)S(1)}, f32[64,8,16]{2,0,1:T(8,128)}, u32[]{:S(2)}) copy-start(f32[64,8,16]{2,0,1:T(8,128)} %get-tuple-element.49) | copy-start | bytes 98308
  258.0 9.5 %copy-start.10 = (f32[64,8,16]{2,0,1:T(8,128)S(1)}, f32[64,8,16]{2,0,1:T(8,128)}, u32[]{:S(2)}) copy-start(f32[64,8,16]{2,0,1:T(8,128)} %get-tuple-element.50) | copy-start | bytes 98308
  275.4 7.8 %copy-start.1 = (bf16[64,8,24,16]{3,0,2,1:T(8,128)(2,1)S(1)}, bf16[64,8,24,16]{3,0,2,1:T(8,128)(2,1)}, u32[]{:S(2)}) copy-start(bf16[64,8,24,16]{3,0,2,1:T(8,128)(2,1)} %get-tuple-element.11) | copy-start | bytes 1179652
  275.4 7.8 %copy-start.2 = (bf16[64,8,24,16]{3,0,2,1:T(8,128)(2,1)S(1)}, bf16[64,8,24,16]{3,0,2,1:T(8,128)(2,1)}, u32[]{:S(2)}) copy-start(bf16[64,8,24,16]{3,0,2,1:T(8,128)(2,1)} %get-tuple-element.12) | copy-start | bytes 1179652
  296.2 2.1 copy-start.7
  306.7 5.5 %copy-start.3 = (f32[2,32,8,1536]{3,2,0,1:T(8,128)S(1)}, f32[2,32,8,1536]{3,2,0,1:T(8,128)}, u32[]{:S(2)}) copy-start(f32[2,32,8,1536]{3,2,0,1:T(8,128)} %copy.70) | copy-start | bytes 9437188
Sparse Core Ops, SparseCore 0:
  9.6 79.6 all-gather.4
  91.5 46.2 all-gather.6
  140.0 79.5 all-gather.8
  221.7 46.2 all-gather.10
where the time goes:
time: 330 us; the launch traced here: 326 us
  waiting for transfers between devices  139 us (42%)
  other arithmetic  58.8 us (18%)
  matrix products  55.7 us (17%)
  local copies, waits for them, and re-layouts  43.2 us (13%)
  starting transfers between devices  15.1 us (5%)
  between operations  14.1 us (4%)
    all_gather x2, waiting for transfers between devices, project_qkv(): lax.all_gather(weight, 'fsdp', axis=1, tiled=True)  73.2 us
    all_to_all x1, waiting for transfers between devices, on_device(): lax.all_to_all(tiles.reshape(count, slots, width), 'fsdp', split_axis=0,...  27.7 us
    all_to_all x1, waiting for transfers between devices, on_device(): lax.all_to_all(hidden, 'fsdp', split_axis=1, concat_axis=0, tiled=True)  25.3 us
    dot_general x2, matrix products, multiply(): return jnp.dot(normed, piece, preferred_element_type=jnp.float32)  22.2 us
    another operation x4, other arithmetic  16.9 us
    dot_general x2, matrix products, attend(): jnp.einsum(score_form, query, key, preferred_element_type=jnp.float32)  15.4 us
    reduce_sum x4, other arithmetic, head_norm(): scale = lax.rsqrt(jnp.mean(values * values, axis=-1, keepdims=True) + EPS)  13.1 us
    convert_element_type x3, local copies, waits for them, and re-layouts, attend(): (mixed / total[..., None]).reshape(qkv.shape[:-1] + (width,))  12.4 us
  transfers between devices with their start and end apart: 6, of which 5 were waited for; matrix products, arithmetic and copies ran while one was open for 46% of the time, Pallas kernels for 0%

commit v1 on v0

v1 whole, which is shorter than its diff:
```python
import functools

import jax
import jax.numpy as jnp
from jax import lax
from jax.experimental import pallas as pl
from jax.experimental.pallas import tpu as pltpu
from jax.sharding import PartitionSpec as P

HEADS = 24
SIZE = 64
EPS = 1e-06
F32 = jnp.float32
BF16 = jnp.bfloat16
NT = (((1,), (1,)), ((), ()))


def params(mib):
    return pltpu.CompilerParams(vmem_limit_bytes=mib * 1024 * 1024)


def one_hot(hot, order_row):
    rows = lax.broadcasted_iota(jnp.int32, (hot, hot), 0)
    return (rows == order_row).astype(BF16)


def select(matrix, values):
    return jnp.dot(matrix, values, preferred_element_type=F32)


def normed(values, gain):
    scale = lax.rsqrt(jnp.mean(values * values, axis=-1, keepdims=True) + EPS)
    return (values * scale * gain).astype(BF16)


def enter_kernel(send_ref, row_ref, gain_ref, tiles_ref, x_ref, xn_ref):
    tiles = tiles_ref[...]
    hot = tiles.shape[0]
    x_ref[...] = select(one_hot(hot, send_ref[...]), tiles).astype(BF16)
    xn_ref[...] = normed(select(one_hot(hot, row_ref[...]), tiles), gain_ref[...])


def turn_kernel(order_ref, gain_ref, h_ref, xn_ref):
    xn = normed(h_ref[...].astype(F32), gain_ref[...])
    xn_ref[...] = select(one_hot(xn.shape[0], order_ref[...]), xn).astype(BF16)


def qkv_kernel(w_ref, xn_ref, out_ref):
    blocks, rows, width = w_ref.shape
    w = w_ref[...].reshape(blocks * rows, width)
    out_ref[...] = lax.dot_general(w, xn_ref[...], NT, preferred_element_type=F32).astype(BF16)


def swap_halves(t):
    return jnp.concatenate([t[16:32], t[:16], t[48:64], t[32:48]], axis=0)


def turned(t, cos, sin, factor):
    scale = lax.rsqrt(jnp.mean(t * t, axis=0, keepdims=True) + EPS) * factor
    return (t * cos + swap_halves(t) * sin) * scale


def attend_kernel(q_ref, k_ref, v_ref, cq_ref, sq_ref, ck_ref, sk_ref, bias_ref, out_ref):
    groups, keys, _ = bias_ref.shape
    for head in range(q_ref.shape[0] // SIZE):
        at = slice(head * SIZE, (head + 1) * SIZE)
        q = turned(q_ref[at, :].astype(F32), cq_ref[...], sq_ref[...], SIZE**-0.5).astype(BF16)
        k = turned(k_ref[at, :].astype(F32), ck_ref[...], sk_ref[...], 1.0)
        k = k.T.astype(BF16)
        v = v_ref[at, :]
        for group in range(groups):
            line = slice(group * keys, (group + 1) * keys)
            s = jnp.dot(k[line], q[:, line], preferred_element_type=F32) + bias_ref[group]
            w = jnp.exp(s - jnp.max(s, axis=0, keepdims=True))
            total = jnp.sum(w, axis=0, keepdims=True)
            mixed = jnp.dot(v[:, line], w.astype(BF16), preferred_element_type=F32)
            out_ref[at, line] = (mixed * (1.0 / total)).astype(BF16)


def out_kernel(order_ref, w_ref, mixed_ref, x_ref, out_ref, held_ref):
    @pl.when(pl.program_id(0) == 0)
    def _():
        pick = one_hot(mixed_ref.shape[1], order_ref[...])
        held_ref[...] = lax.dot_general(pick, mixed_ref[...], NT, preferred_element_type=F32).astype(BF16)

    blocks, rows, width = w_ref.shape
    w = w_ref[...].reshape(blocks * rows, width)
    add = lax.dot_general(held_ref[...], w, NT, preferred_element_type=F32)
    out_ref[...] = (x_ref[...].astype(F32) + add).astype(BF16)


def enter(tiles, send_order, row_order, gain):
    shape = jax.ShapeDtypeStruct(tiles.shape, BF16)
    return pl.pallas_call(
        enter_kernel, out_shape=(shape, shape), compiler_params=params(40), name="enter"
    )(send_order, row_order, gain, tiles)


def turn(h, order, gain):
    return pl.pallas_call(
        turn_kernel, out_shape=jax.ShapeDtypeStruct(h.shape, BF16), compiler_params=params(40), name="turn"
    )(order, gain, h)


def qkv_of(weights, xn):
    parts, _, width = weights.shape
    tokens = xn.shape[0]
    step, rows = 4, 3 * width // parts
    return pl.pallas_call(
        qkv_kernel,
        grid=(parts // step,),
        in_specs=[
            pl.BlockSpec((step, rows, width), lambda i: (i, 0, 0)),
            pl.BlockSpec((tokens, width), lambda i: (0, 0)),
        ],
        out_specs=pl.BlockSpec((step * rows, tokens), lambda i: (i, 0)),
        out_shape=jax.ShapeDtypeStruct((3 * width, tokens), BF16),
        compiler_params=params(40),
        name="qkv",
    )(weights, xn)


def attend(qkv, tables, bias, heads_step):
    width3, tokens = qkv.shape
    rows = heads_step * SIZE
    steps = HEADS // heads_step

    def part(j):
        return pl.BlockSpec((rows, tokens), lambda i, j=j: (j * steps + i, 0))

    table = pl.BlockSpec((SIZE, tokens), lambda i: (0, 0))
    return pl.pallas_call(
        attend_kernel,
        grid=(steps,),
        in_specs=[part(0), part(1), part(2), table, table, table, table, pl.BlockSpec(bias.shape, lambda i: (0, 0, 0))],
        out_specs=part(0),
        out_shape=jax.ShapeDtypeStruct((width3 // 3, tokens), BF16),
        compiler_params=params(40),
        name="attend",
    )(qkv, qkv, qkv, *tables, bias)


def out_of(weights, mixed, x, order):
    parts, rows4, width = weights.shape
    tokens = x.shape[0]
    step, rows = 8, rows4 // 4
    return pl.pallas_call(
        out_kernel,
        grid=(parts // step,),
        in_specs=[
            pl.BlockSpec((1, tokens), lambda i: (0, 0)),
            pl.BlockSpec((step, rows, width), lambda i: (i, 3, 0)),
            pl.BlockSpec((width, tokens), lambda i: (0, 0)),
            pl.BlockSpec((tokens, step * rows), lambda i: (0, i)),
        ],
        out_specs=pl.BlockSpec((tokens, step * rows), lambda i: (0, i)),
        out_shape=jax.ShapeDtypeStruct((tokens, width), BF16),
        scratch_shapes=[pltpu.VMEM((tokens, width), BF16)],
        compiler_params=params(40),
        name="project",
    )(order, weights, mixed, x)


def rotary_tables(gains, rows_pos, cols_pos):
    quarter = SIZE // 4
    freq = 10000.0 ** (-jnp.arange(quarter).astype(F32) / quarter)
    by_row = freq[:, None] * rows_pos.astype(F32)[None, :]
    by_col = freq[:, None] * cols_pos.astype(F32)[None, :]
    cr, sr, cc, sc = jnp.cos(by_row), jnp.sin(by_row), jnp.cos(by_col), jnp.sin(by_col)
    cosine = jnp.concatenate([cr, cr, cc, cc], axis=0)
    sine = jnp.concatenate([-sr, sr, -sc, sc], axis=0)
    out = []
    for gain in (gains[0], gains[1]):
        other = jnp.concatenate([gain[16:32], gain[:16], gain[48:64], gain[32:48]])
        out += [gain[:, None] * cosine, other[:, None] * sine]
    return out


def on_device(tiles, tile_cell, tissue, norm_gain, qk_gain, row_qkv, row_out, col_qkv, col_out):
    count = lax.axis_size("fsdp")
    index = lax.axis_index("fsdp")
    tokens, width = tiles.shape
    slots = tokens // count
    grid_rows, columns = tissue.shape
    rows_dev = grid_rows // count
    cols_dev = columns // count

    def gather(qkv, out):
        return lax.all_gather(jnp.concatenate([qkv.T, out.T], axis=0), "fsdp", axis=0, tiled=False)

    row_w = gather(row_qkv, row_out)
    col_w = gather(col_qkv, col_out)

    arrived = lax.all_to_all(
        tiles.reshape(count, slots, width), "fsdp", split_axis=0, concat_axis=0, tiled=True
    ).reshape(tokens, width)
    table_cell = lax.dynamic_index_in_dim(tile_cell.reshape(count, count, slots), index, 1, keepdims=False)
    row_base = index * rows_dev
    col_base = index * cols_dev
    local = (table_cell - row_base * columns).reshape(1, tokens)
    r, c = local // columns, local % columns
    send = (c // cols_dev) * (rows_dev * cols_dev) + r * cols_dev + c % cols_dev

    token = jnp.arange(tokens, dtype=jnp.int32)
    row_tables = rotary_tables(qk_gain[0], row_base + token // columns, token % columns)
    live = lax.dynamic_slice_in_dim(tissue, row_base, rows_dev, 0) > 0
    at = jnp.arange(columns)
    allow = live[:, :, None] | (at[:, None] == at[None, :])[None]
    row_bias = jnp.where(allow, 0.0, -1e30).astype(F32)

    x, xn = enter(arrived, send, local, norm_gain[0:1])
    mixed = attend(qkv_of(row_w, xn), row_tables, row_bias, 2)
    t_c, t_r = token % columns, token // columns
    send_of_row = (t_c // cols_dev) * (rows_dev * cols_dev) + t_r * cols_dev + t_c % cols_dev
    h = out_of(row_w, mixed, x, send_of_row[None, :])
    flat = lax.all_to_all(
        h.reshape(count, slots, width), "fsdp", split_axis=0, concat_axis=0, tiled=True
    ).reshape(tokens, width)

    turned_of = (token % cols_dev) * grid_rows + token // cols_dev
    back_of = (token % grid_rows) * cols_dev + token // grid_rows
    col_tables = rotary_tables(qk_gain[1], token % grid_rows, col_base + token // grid_rows)
    live = lax.dynamic_slice_in_dim(tissue, col_base, cols_dev, 1).T.reshape(-1) > 0
    pair = 2 * grid_rows
    at = jnp.arange(pair)
    same = (at[:, None] // grid_rows) == (at[None, :] // grid_rows)
    allow = (live.reshape(-1, pair)[:, :, None] & same[None]) | (at[:, None] == at[None, :])[None]
    col_bias = jnp.where(allow, 0.0, -1e30).astype(F32)

    xn = turn(flat, turned_of[None, :], norm_gain[1:2])
    mixed = attend(qkv_of(col_w, xn), col_tables, col_bias, 2)
    result = out_of(col_w, mixed, flat, back_of[None, :])
    return result.reshape(grid_rows, cols_dev, width)


def solution(mesh):
    return jax.shard_map(
        on_device,
        mesh=mesh,
        in_specs=(
            P(("slide", "fsdp"), None),
            P("slide"),
            P("slide", None),
            P(),
            P(),
            P(None, "fsdp"),
            P(None, "fsdp"),
            P(None, "fsdp"),
            P(None, "fsdp"),
        ),
        out_specs=P("slide", "fsdp", None),
        check_vma=False,
    )
```

time: 330 us -> 231 us (0.70); the launches traced: 326 us -> 231 us
  Pallas kernels: 0 us -> 64.5 us
  matrix products: 55.7 us -> 0 us
  other arithmetic: 58.8 us -> 5.93 us
  local copies, waits for them, and re-layouts: 43.2 us -> 4.27 us
  waiting for transfers between devices: 139 us -> 127 us
    pallas_call x0 -> x8, Pallas kernels: none -> 64.5 us  [the longest x2 23.7 us: qkv_of(): pl.pallas_call(qkv_kernel, grid=(parts // step,), in_specs=[pl.BlockSpec(...]
    dot_general x8 -> x0, matrix products: 55.7 us -> none  [the longest x2 22.2 us: multiply(): return jnp.dot(normed, piece, preferred_element_type=jnp.float32)]
    convert_element_type x8 -> x0, local copies, waits for them, and re-layouts: 28.2 us -> none  [the longest x3 12.4 us: attend(): (mixed / total[..., None]).reshape(qkv.shape[:-1] + (width,))]
    all_gather x4 -> x2, waiting for transfers between devices: 83.5 us -> 62.9 us  [gather(): lax.all_gather(jnp.concatenate([qkv.T, out.T], axis=0), 'fsdp', axis=0, t...]
    reduce_sum x8 -> x0, other arithmetic: 20.4 us -> none  [the longest x4 13.1 us: head_norm(): scale = lax.rsqrt(jnp.mean(values * values, axis=-1, keepdims=True) + EPS)]
    another operation x4 -> x0, other arithmetic: 16.9 us -> none
    all_to_all x1, waiting for transfers between devices: 25.3 us -> 34.8 us  [on_device(): lax.all_to_all(h.reshape(count, slots, width), 'fsdp', split_axis=0, conc...]
    mul x3 -> x4, other arithmetic: 10.6 us -> 1.7 us  [rotary_tables(): out += [gain[:, None] * cosine, other[:, None] * sine]]
  transfers between devices with their start and end apart: 6 -> 4, of which waited for: 5 -> 4; matrix products, arithmetic and copies ran while one was open for 46% -> 2% of each run, Pallas kernels for 0% -> 17%
where the time goes in v1:
time: 231 us
  waiting for transfers between devices  127 us (55%)
  Pallas kernels  64.5 us (28%)
  starting transfers between devices  15 us (6%)
  between operations  13.7 us (6%)
  other arithmetic  5.93 us (3%)
  local copies, waits for them, and re-layouts  4.27 us (2%)
    all_gather x2, waiting for transfers between devices, gather(): lax.all_gather(jnp.concatenate([qkv.T, out.T], axis=0), 'fsdp', axis=0, t...  62.9 us
    all_to_all x1, waiting for transfers between devices, on_device(): lax.all_to_all(h.reshape(count, slots, width), 'fsdp', split_axis=0, conc...  34.8 us
    all_to_all x1, waiting for transfers between devices, on_device(): lax.all_to_all(tiles.reshape(count, slots, width), 'fsdp', split_axis=0,...  29.4 us
    pallas_call x2, Pallas kernels, qkv_of(): pl.pallas_call(qkv_kernel, grid=(parts // step,), in_specs=[pl.BlockSpec(...  23.7 us
    pallas_call x2, Pallas kernels, attend(): pl.pallas_call(attend_kernel, grid=(steps,), in_specs=[part(0), part(1),...  22.1 us
    pallas_call x2, Pallas kernels, out_of(): pl.pallas_call(out_kernel, grid=(parts // step,), in_specs=[pl.BlockSpec(...  15.3 us
    all_to_all x1, starting transfers between devices, on_device(): lax.all_to_all(tiles.reshape(count, slots, width), 'fsdp', split_axis=0,...  9.73 us
    all_to_all x1, starting transfers between devices, on_device(): lax.all_to_all(h.reshape(count, slots, width), 'fsdp', split_axis=0, conc...  5.25 us
  transfers between devices with their start and end apart: 4, of which 4 were waited for; matrix products, arithmetic and copies ran while one was open for 2% of the time, Pallas kernels for 17%

profile of v1, /device:TPU:1, one launch (start us, length us, event | category | flops | bytes accessed | tf_op | source)
XLA Modules:
  0.0 230.5 jit_solution(12868543517113429695)
XLA Ops:
  6.5 2.0 pad_maximum_fusion.1
  8.6 0.9 pad_maximum_fusion
  9.6 9.7 %all-to-all-start = ((bf16[32,16,1536]{2,1,0:T(8,128)(2,1)}), bf16[32,16,1536]{2,1,0:T(8,128)(2,1)S(1)}, u32[]{:S(2)}, u32[]{:S(2)}) async-start(bf16[32,16,1536]{2,1,0:T(8,128)(2,1)} %bitcast.6), calls=%async_computation | async-start | bytes 3145728 | tf_op jit(solution)/shard_map/all_to_all | solution.py:194
  19.3 0.2 reshape.659
  20.0 0.5 fusion.11
  20.8 0.1 or_select_fusion.bias_ref
  20.9 29.4 %all-to-all-done = bf16[32,16,1536]{2,1,0:T(8,128)(2,1)S(1)} async-done(((bf16[32,16,1536]{2,1,0:T(8,128)(2,1)}), bf16[32,16,1536]{2,1,0:T(8,128)(2,1)S(1)}, u32[]{:S(2)}, u32[]{:S(2)}) %all-to-all-start) | async-done | bytes 1572896 | tf_op jit(solution)/shard_map/all_to_all | solution.py:194
  50.3 2.1 enter.1
  52.4 1.2 copy-done
  53.5 1.1 copy-done.2
  54.7 47.0 %all-gather.7.cloned.1.call-done = bf16[6144,1536]{1,0:T(8,128)(2,1)} async-done(((bf16[192,1536]{1,0:T(8,128)(2,1)}), bf16[6144,1536]{1,0:T(8,128)(2,1)}) %all-gather.7.cloned.1.call-update) | async-done | bytes 18874384 | tf_op jit(solution)/shard_map/all_gather | solution.py:189
  101.7 1.4 copy-done.3
  103.1 11.9 %qkv.2.q_ref.k_ref.v_ref = bf16[4608,512]{1,0:T(8,128)(2,1)S(1)} custom-call(bf16[32,192,1536]{2,1,0:T(8,128)(2,1)} %bitcast.58, bf16[512,1536]{1,0:T(8,128)(2,1)S(1)} %copy-done.3), custom_call_target="tpu_custom_call" | custom-call | tf_op jit(solution)/shard_map/qkv/pallas_call | solution.py:109
  115.0 15.7 %attend.2.mixed_ref = bf16[1536,512]{1,0:T(8,128)(2,1)S(1)} custom-call(bf16[4608,512]{1,0:T(8,128)(2,1)S(1)} %qkv.2.q_ref.k_ref.v_ref, bf16[4608,512]{1,0:T(8,128)(2,1)S(1)} %qkv.2.q_ref.k_ref.v_ref, bf16[4608,512]{1,0:T(8,128)(2,1)S(1)} %qkv.2.q_ref.k_ref.v_ref, f32[64,512]{1,0:T(8,128)S(1)} %get-tuple-element.16.cq_ref, ...), custom_call_target="tpu_custom_call" | custom-call | tf_op jit(solution)/shard_map/attend/pallas_call | solution.py:132
  130.7 7.6 %project.2 = bf16[512,1536]{1,0:T(8,128)(2,1)} custom-call(s32[1,512]{1,0:T(1,128)S(1)} %fusion.19.order_ref, bf16[32,192,1536]{2,1,0:T(8,128)(2,1)} %bitcast.59, bf16[1536,512]{1,0:T(8,128)(2,1)S(1)} %attend.2.mixed_ref, bf16[512,1536]{1,0:T(8,128)(2,1)S(1)} %copy-done.1), custom_call_target="tpu_custom_call" | custom-call | tf_op jit(solution)/shard_map/project/pallas_call | solution.py:147
  138.3 5.2 %all-to-all-start.1 = ((bf16[32,16,1536]{2,1,0:T(8,128)(2,1)}), bf16[32,16,1536]{2,1,0:T(8,128)(2,1)S(1)}, u32[]{:S(2)}, u32[]{:S(2)}) async-start(bf16[32,16,1536]{2,1,0:T(8,128)(2,1)} %bitcast.18), calls=%async_computation.1 | async-start | bytes 3145728 | tf_op jit(solution)/shard_map/all_to_all | solution.py:216
  144.0 0.8 fusion
  144.8 0.7 fusion.4
  145.7 34.8 %all-to-all-done.1 = bf16[32,16,1536]{2,1,0:T(8,128)(2,1)S(1)} async-done(((bf16[32,16,1536]{2,1,0:T(8,128)(2,1)}), bf16[32,16,1536]{2,1,0:T(8,128)(2,1)S(1)}, u32[]{:S(2)}, u32[]{:S(2)}) %all-to-all-start.1) | async-done | bytes 1572896 | tf_op jit(solution)/shard_map/all_to_all | solution.py:216
  180.5 1.4 turn.1.xn_ref
  181.9 15.9 %all-gather.5.cloned.1.call-done = bf16[6144,1536]{1,0:T(8,128)(2,1)} async-done(((bf16[192,1536]{1,0:T(8,128)(2,1)}), bf16[6144,1536]{1,0:T(8,128)(2,1)}) %all-gather.5.cloned.1.call-update) | async-done | bytes 18874384 | tf_op jit(solution)/shard_map/all_gather | solution.py:189
  197.8 11.8 %qkv.3.q_ref.k_ref.v_ref = bf16[4608,512]{1,0:T(8,128)(2,1)S(1)} custom-call(bf16[32,192,1536]{2,1,0:T(8,128)(2,1)} %bitcast.56, bf16[512,1536]{1,0:T(8,128)(2,1)S(1)} %turn.1.xn_ref), custom_call_target="tpu_custom_call" | custom-call | tf_op jit(solution)/shard_map/qkv/pallas_call | solution.py:109
  209.6 6.4 %attend.3.mixed_ref = bf16[1536,512]{1,0:T(8,128)(2,1)S(1)} custom-call(bf16[4608,512]{1,0:T(8,128)(2,1)S(1)} %qkv.3.q_ref.k_ref.v_ref, bf16[4608,512]{1,0:T(8,128)(2,1)S(1)} %qkv.3.q_ref.k_ref.v_ref, bf16[4608,512]{1,0:T(8,128)(2,1)S(1)} %qkv.3.q_ref.k_ref.v_ref, f32[64,512]{1,0:T(8,128)S(1)} %copy-done.6, f32[64,512]{1,0:T(8,128)S(1)} %copy-done.4, ...), custom_call_target="tpu_custom_call" | custom-call | tf_op jit(solution)/shard_map/attend/pallas_call | solution.py:132
  216.0 7.6 %project.3 = bf16[512,1536]{1,0:T(8,128)(2,1)} custom-call(s32[1,512]{1,0:T(1,128)S(1)} %fusion.16.order_ref, bf16[32,192,1536]{2,1,0:T(8,128)(2,1)} %bitcast.57, bf16[1536,512]{1,0:T(8,128)(2,1)S(1)} %attend.3.mixed_ref, bf16[512,1536]{1,0:T(8,128)(2,1)S(1)} %bitcast.54), custom_call_target="tpu_custom_call" | custom-call | tf_op jit(solution)/shard_map/project/pallas_call | solution.py:147
  (51 shorter events, 1.3 us)
Async XLA Ops:
  6.5 2.1 copy-start.7
  6.5 2.1 copy-start.8
  6.5 95.1 %all-gather.7.cloned.1.call-start = ((), (), s32[]{:S(2)}) async-start(), calls=%async_computation.3 | async-start | bytes 19464192 | tf_op jit(solution)/shard_map/all_gather | solution.py:189
  8.6 189.2 %all-gather.5.cloned.1.call-start = ((), (), s32[]{:S(2)}) async-start(), calls=%async_computation.2 | async-start | bytes 19464192 | tf_op jit(solution)/shard_map/all_gather | solution.py:189
  9.5 9.8 %copy-start.9 = (s32[16384]{0:T(1024)S(1)}, s32[16384]{0:T(1024)}, u32[]{:S(2)}) copy-start(s32[16384]{0:T(1024)} %param.10) | copy-start | bytes 196612
  9.5 10.1 %copy-start.11 = (s32[64,256]{1,0:T(8,128)S(1)}, s32[64,256]{1,0:T(8,128)}, u32[]{:S(2)}) copy-start(s32[64,256]{1,0:T(8,128)} %param.11) | copy-start | bytes 196612
  9.5 10.1 %copy-start.10 = (f32[2,2,64]{2,1,0:T(2,128)S(1)}, f32[2,2,64]{2,1,0:T(2,128)}, u32[]{:S(2)}) copy-start(f32[2,2,64]{2,1,0:T(2,128)} %param.13) | copy-start | bytes 3076
  9.6 40.7 %all-to-all-start = ((bf16[32,16,1536]{2,1,0:T(8,128)(2,1)}), bf16[32,16,1536]{2,1,0:T(8,128)(2,1)S(1)}, u32[]{:S(2)}, u32[]{:S(2)}) async-start(bf16[32,16,1536]{2,1,0:T(8,128)(2,1)} %bitcast.6), calls=%async_computation | async-start | bytes 3145728 | tf_op jit(solution)/shard_map/all_to_all | solution.py:194
  19.3 1.6 copy-start.12
  52.4 1.2 copy-start
  53.5 1.1 copy-start.2
  101.7 1.4 copy-start.3
  115.0 15.7 %copy-start.1 = (bf16[512,1536]{1,0:T(8,128)(2,1)S(1)}, bf16[512,1536]{1,0:T(8,128)(2,1)}, u32[]{:S(2)}) copy-start(bf16[512,1536]{1,0:T(8,128)(2,1)} %copy-done) | copy-start | bytes 4718596
  138.3 42.2 %all-to-all-start.1 = ((bf16[32,16,1536]{2,1,0:T(8,128)(2,1)}), bf16[32,16,1536]{2,1,0:T(8,128)(2,1)S(1)}, u32[]{:S(2)}, u32[]{:S(2)}) async-start(bf16[32,16,1536]{2,1,0:T(8,128)(2,1)} %bitcast.18), calls=%async_computation.1 | async-start | bytes 3145728 | tf_op jit(solution)/shard_map/all_to_all | solution.py:216
  197.8 11.8 %copy-start.4 = (f32[64,512]{1,0:T(8,128)S(1)}, f32[64,512]{1,0:T(8,128)}, u32[]{:S(2)}) copy-start(f32[64,512]{1,0:T(8,128)} %get-tuple-element.10.sq_ref) | copy-start | bytes 393220
  197.8 11.8 %copy-start.5 = (f32[64,512]{1,0:T(8,128)S(1)}, f32[64,512]{1,0:T(8,128)}, u32[]{:S(2)}) copy-start(f32[64,512]{1,0:T(8,128)} %get-tuple-element.13.ck_ref) | copy-start | bytes 393220
  197.8 11.8 %copy-start.6 = (f32[64,512]{1,0:T(8,128)S(1)}, f32[64,512]{1,0:T(8,128)}, u32[]{:S(2)}) copy-start(f32[64,512]{1,0:T(8,128)} %get-tuple-element.14.cq_ref) | copy-start | bytes 393220
Sparse Core Ops, SparseCore 0:
  9.6 92.0 all-gather.6
  103.9 93.8 all-gather.4
